TPU v7x, 256 devices: a whole 4x4x8 slice. The times are simulated.
256 devices in a mesh: chain: 8 (over y, core), cols: 32 (over x, z).
Axes of the slice: x: 4, y: 4, z: 8, core: 2. Of those that a mesh axis runs over, the one named last changes fastest.
Arguments:
- factor: float32 [4608, 4608], P(('chain', 'cols')), may hold values from -2 to 2, as said below
- right_side: float32 [4608, 16384], P('chain', 'cols'), may hold values from -6 to 6
- occ_order: int32 [64], replicated, may hold values from 0 to 63, each once
- cabs_order: int32 [256], replicated, may hold values from 0 to 255, each once
Outputs:
- fitted: float32 [64, 256, 4608], P('cols', None, 'chain')
Inputs may be any that keep to these rules, and one draw needn't show every extreme that they name: factor is lower triangular: zero above the diagonal, its diagonal between 1 and 2.
All inputs are finite; a program needn't handle non-finite values.
Results may differ from a plain program's by a relative error of at most 0.00017.
Values sent between devices are 32-bit elements; how exact they have to be, the bound alone decides.
No kernel may reach another device: no remote copies, remote signals or barrier semaphores. Data moves between devices by JAX's collectives and lax.ppermute only.
A program may use at most 128 MiB of HBM per device.

v0:
```python
import jax
import jax.numpy as jnp
from jax import lax
from jax.sharding import PartitionSpec as P


def from_root(value, axis, root):
    return lax.dynamic_index_in_dim(lax.all_gather(value, axis), root, 0, keepdims=False)


def product(left, right):
    return jnp.dot(left, right, precision=lax.Precision.HIGHEST, preferred_element_type=jnp.float32)


def per_device(factor, right_side, occ_order, cabs_order):
    chain_size = lax.axis_size("chain")
    position = lax.axis_index("chain")
    factor_row = lax.all_gather(factor, "cols", axis=0, tiled=True)
    aux_rows = factor_row.shape[0]
    diag_block = lax.dynamic_slice_in_dim(factor_row, position * aux_rows, aux_rows, 1)
    identity = jnp.eye(aux_rows, dtype=jnp.float32)
    inverse = jax.scipy.linalg.solve_triangular(diag_block, identity, lower=True)

    def settle(residual):
        return product(inverse, residual)

    def blank(residual):
        return jnp.zeros_like(residual)

    residual = right_side
    solution = jnp.zeros_like(right_side)
    for section in range(chain_size):
        solved = lax.cond(position == section, settle, blank, residual)
        solution = solution + solved
        if section + 1 < chain_size:
            arrived = from_root(solved, "chain", section)
            coupling = factor_row[:, section * aux_rows : (section + 1) * aux_rows]

            def lower_block(current, arrived=arrived, coupling=coupling):
                return current - product(coupling, arrived)

            def keep_block(current):
                return current

            residual = lax.cond(position > section, lower_block, keep_block, residual)
    occ_total = occ_order.shape[0]
    cabs_local = right_side.shape[1] // occ_total
    cols_size = lax.axis_size("cols")
    occ_local = occ_total // cols_size
    grid = solution.reshape(aux_rows, cabs_local, occ_total)
    grid = jnp.take(grid, occ_order, axis=2)
    grid = grid.reshape(aux_rows, cabs_local, cols_size, occ_local)
    grid = jnp.transpose(grid, (2, 3, 1, 0))
    moved = jnp.take(
        lax.all_to_all(grid, "cols", split_axis=0, concat_axis=2, tiled=True), cabs_order, axis=2
    )
    return moved.reshape(occ_local, moved.shape[2], aux_rows)


def solution(mesh):
    in_specs = (P(("chain", "cols"), None), P("chain", "cols"), P(), P())
    out_specs = P("cols", None, "chain")
    return jax.shard_map(
        per_device, mesh=mesh, in_specs=in_specs, out_specs=out_specs, check_vma=False
    )
```

profile of v0, /device:TPU:33, one launch (start us, length us, event | category | flops | bytes accessed | tf_op | source)
XLA Modules:
  0.0 740.3 jit_solution(2091140109980776723)
XLA Ops:
  6.5 1.3 copy.126
  8.1 1.2 fusion.68
  9.3 128.3 %all-gather.31.cloned.1.call-done = f32[32,18,4608]{2,1,0:T(8,128)} async-done(((f32[1,18,4608]{2,1,0:T(8,128)}), f32[32,18,4608]{2,1,0:T(8,128)}) %all-gather.31.cloned.1.call-update) | async-done | bytes 10616848 | tf_op jit(solution)/shard_map/all_gather | solution.py:18
  137.6 11.4 %reshape.89 = f32[576,4608]{1,0:T(8,128)} reshape(f32[32,18,4608]{2,1,0:T(8,128)} %all-gather.31.cloned.1.call-done) | data formatting | bytes 21233664
  149.0 1.8 dynamic-slice_select_fusion
  150.7 10.5 %while.1 = (s32[]{:T(128)}, f32[576,576]{1,0:T(8,128)S(1)}, s32[4,2]{0,1:T(2,128)S(1)}, f32[4,128,128]{2,1,0:T(8,128)}, s32[]{:T(128)}) while((s32[]{:T(128)}, f32[576,576]{1,0:T(8,128)S(1)}, s32[4,2]{0,1:T(2,128)S(1)}, f32[4,128,128]{2,1,0:T(8,128)}, s32[]{:T(128)}) %tuple.169), condition=%wide.while_cond, body=%wide.while_body.sunk | while | flops 2 | bytes 132705 | solution.py:22
  150.8 0.6 fusion.114
  151.4 2.0 bitcast_dynamic-update-slice_fusion.2
  153.4 0.6 fusion.114
  154.0 2.0 bitcast_dynamic-update-slice_fusion.2
  156.1 0.6 fusion.114
  156.7 2.0 bitcast_dynamic-update-slice_fusion.2
  158.7 0.6 fusion.114
  159.3 2.0 bitcast_dynamic-update-slice_fusion.2
  161.4 1.2 pad_maximum_fusion
  162.6 49.8 %custom-call.4 = f32[5,128,128]{1,2,0:T(8,128)} custom-call(f32[5,128,128]{2,1,0:T(8,128)S(1)} %pad_maximum_fusion), custom_call_target="InvertDiagBlocksLowerTriangular" | custom-call | tf_op jit(solution)/shard_map/jit(_solve_triangular)/triangular_solve | solution.py:22
  212.3 1.2 constant_dynamic-update-slice_fusion.3
  213.6 1.4 convolution_subtract_fusion.1
  215.0 1.3 constant_dynamic-update-slice_fusion.2
  216.3 1.5 convolution_subtract_fusion
  217.8 0.4 constant_dynamic-update-slice_fusion.1
  218.2 1.9 convolution_subtract_fusion.2
  220.1 0.4 constant_dynamic-update-slice_fusion
  220.5 2.0 fusion.57
  222.5 0.4 convolution_dynamic-update-slice_fusion
  222.9 1.2 conditional.15
  222.9 1.2 broadcast.60
  224.1 56.9 %all-gather.17.cloned.1.call-done = f32[4608,512]{1,0:T(8,128)} async-done(((f32[576,512]{1,0:T(8,128)}), f32[4608,512]{1,0:T(8,128)}) %all-gather.17.cloned.1.call-update) | async-done | bytes 9437200 | tf_op jit(solution)/shard_map/all_gather | solution.py:8
  281.0 5.0 conditional.16
  281.2 4.8 fusion.2
  286.0 4.1 conditional.17
  286.0 4.1 fusion.84
  290.2 55.5 %all-gather.19.cloned.1.call-done = f32[4608,512]{1,0:T(8,128)} async-done(((f32[576,512]{1,0:T(8,128)}), f32[4608,512]{1,0:T(8,128)}) %all-gather.19.cloned.1.call-update) | async-done | bytes 9437200 | tf_op jit(solution)/shard_map/all_gather | solution.py:8
  345.7 1.2 conditional.19
  345.7 1.2 broadcast.62
  347.0 63.7 %all-gather.21.cloned.1.call-done = f32[4608,512]{1,0:T(8,128)} async-done(((f32[576,512]{1,0:T(8,128)}), f32[4608,512]{1,0:T(8,128)}) %all-gather.21.cloned.1.call-update) | async-done | bytes 9437200 | tf_op jit(solution)/shard_map/all_gather | solution.py:8
  410.7 0.4 conditional.20
  411.1 1.2 conditional.21
  411.1 1.2 broadcast.63
  412.4 63.4 %all-gather.23.cloned.1.call-done = f32[4608,512]{1,0:T(8,128)} async-done(((f32[576,512]{1,0:T(8,128)}), f32[4608,512]{1,0:T(8,128)}) %all-gather.23.cloned.1.call-update) | async-done | bytes 9437200 | tf_op jit(solution)/shard_map/all_gather | solution.py:8
  475.8 1.2 conditional.23
  475.8 1.2 broadcast.64
  477.1 64.9 %all-gather.25.cloned.1.call-done = f32[4608,512]{1,0:T(8,128)} async-done(((f32[576,512]{1,0:T(8,128)}), f32[4608,512]{1,0:T(8,128)}) %all-gather.25.cloned.1.call-update) | async-done | bytes 9437200 | tf_op jit(solution)/shard_map/all_gather | solution.py:8
  542.0 0.2 conditional.24
  542.1 1.2 conditional.25
  542.1 1.2 broadcast.65
  543.4 64.6 %all-gather.27.cloned.1.call-done = f32[4608,512]{1,0:T(8,128)} async-done(((f32[576,512]{1,0:T(8,128)}), f32[4608,512]{1,0:T(8,128)}) %all-gather.27.cloned.1.call-update) | async-done | bytes 9437200 | tf_op jit(solution)/shard_map/all_gather | solution.py:8
  608.0 1.2 conditional.27
  608.0 1.2 broadcast.66
  609.4 63.8 %all-gather.29.cloned.1.call-done = f32[4608,512]{1,0:T(8,128)} async-done(((f32[576,512]{1,0:T(8,128)}), f32[4608,512]{1,0:T(8,128)}) %all-gather.29.cloned.1.call-update) | async-done | bytes 9437200 | tf_op jit(solution)/shard_map/all_gather | solution.py:8
  673.2 0.2 conditional.28
  673.4 1.2 conditional.29
  673.4 1.2 broadcast.67
  674.6 4.9 add_add_fusion
  679.5 0.4 copy.67
  679.9 0.8 copy.68
  680.7 0.7 gather_fusion
  681.3 1.2 select_bitcast_fusion.1
  682.6 9.9 %all-to-all-start = ((f32[32,2,8,576]{3,2,1,0:T(8,128)}), f32[32,2,8,576]{3,2,1,0:T(8,128)S(1)}, u32[]{:S(2)}, u32[]{:S(2)}) async-start(f32[32,2,8,576]{3,2,1,0:T(8,128)} %select_bitcast_fusion.1), calls=%async_computation | async-start | bytes 2621440 | tf_op jit(solution)/shard_map/all_to_all | solution.py:55
  692.5 34.0 %all-to-all-done = f32[32,2,8,576]{3,2,1,0:T(8,128)S(1)} async-done(((f32[32,2,8,576]{3,2,1,0:T(8,128)}), f32[32,2,8,576]{3,2,1,0:T(8,128)S(1)}, u32[]{:S(2)}, u32[]{:S(2)}) %all-to-all-start) | async-done | bytes 1179680 | tf_op jit(solution)/shard_map/all_to_all | solution.py:55
  726.5 1.0 copy.70
  727.5 2.2 gather_fusion.1
  729.7 1.1 select_bitcast_fusion
  730.8 2.2 copy.71
  (48 shorter events, 1.2 us)
Async XLA Ops:
  6.5 131.1 %all-gather.31.cloned.1.call-start = ((), (), s32[]{:S(2)}) async-start(), calls=%async_computation.8 | async-start | bytes 14598144 | tf_op jit(solution)/shard_map/all_gather | solution.py:18
  7.8 273.2 %all-gather.17.cloned.1.call-start = ((), (), s32[]{:S(2)}) async-start(), calls=%async_computation.1 | async-start | bytes 10616832 | tf_op jit(solution)/shard_map/all_gather | solution.py:8
  161.3 1.3 copy-start.1
  212.3 4.0 copy-start
  215.0 2.9 copy-start.2
  224.1 121.7 %all-gather.19.cloned.1.call-start = ((), (), s32[]{:S(2)}) async-start(), calls=%async_computation.2 | async-start | bytes 10616832 | tf_op jit(solution)/shard_map/all_gather | solution.py:8
  290.1 120.5 %all-gather.21.cloned.1.call-start = ((), (), s32[]{:S(2)}) async-start(), calls=%async_computation.3 | async-start | bytes 10616832 | tf_op jit(solution)/shard_map/all_gather | solution.py:8
  347.0 128.8 %all-gather.23.cloned.1.call-start = ((), (), s32[]{:S(2)}) async-start(), calls=%async_computation.4 | async-start | bytes 10616832 | tf_op jit(solution)/shard_map/all_gather | solution.py:8
  412.4 129.6 %all-gather.25.cloned.1.call-start = ((), (), s32[]{:S(2)}) async-start(), calls=%async_computation.5 | async-start | bytes 10616832 | tf_op jit(solution)/shard_map/all_gather | solution.py:8
  477.0 131.0 %all-gather.27.cloned.1.call-start = ((), (), s32[]{:S(2)}) async-start(), calls=%async_computation.6 | async-start | bytes 10616832 | tf_op jit(solution)/shard_map/all_gather | solution.py:8
  543.3 129.9 %all-gather.29.cloned.1.call-start = ((), (), s32[]{:S(2)}) async-start(), calls=%async_computation.7 | async-start | bytes 10616832 | tf_op jit(solution)/shard_map/all_gather | solution.py:8
  608.0 1.2 copy-start.4
  608.0 1.3 copy-start.3
  682.6 43.8 %all-to-all-start = ((f32[32,2,8,576]{3,2,1,0:T(8,128)}), f32[32,2,8,576]{3,2,1,0:T(8,128)S(1)}, u32[]{:S(2)}, u32[]{:S(2)}) async-start(f32[32,2,8,576]{3,2,1,0:T(8,128)} %select_bitcast_fusion.1), calls=%async_computation | async-start | bytes 2621440 | tf_op jit(solution)/shard_map/all_to_all | solution.py:55
Sparse Core Ops, SparseCore 0:
  9.9 127.6 all-gather.30
  224.2 56.7 all-gather.16
  290.3 55.4 all-gather.18
  347.4 63.2 all-gather.20
  412.5 63.2 all-gather.22
  477.5 64.4 all-gather.24
  543.8 64.1 all-gather.26
  609.9 63.3 all-gather.28
where the time goes:
time: 749 us; the launch traced here: 740 us
  waiting for transfers between devices  595 us (79%)
  other arithmetic  61.4 us (8%)
  local copies, waits for them, and re-layouts  38.8 us (5%)
  matrix products  19.3 us (3%)
  between operations  14.3 us (2%)
  starting transfers between devices  10.1 us (1%)
    all_gather x7, waiting for transfers between devices, from_root(): lax.all_gather(value, axis)  433 us
    all_gather x1, waiting for transfers between devices, per_device(): factor_row = lax.all_gather(factor, 'cols', axis=0, tiled=True)  128 us
    another operation x7, other arithmetic, per_device(): jax.scipy.linalg.solve_triangular(diag_block, identity, lower=True)  52.8 us
    all_to_all x1, waiting for transfers between devices, per_device(): lax.all_to_all(grid, 'cols', split_axis=0, concat_axis=2, tiled=True)  34 us
    another operation x19, local copies, waits for them, and re-layouts  18.8 us
  transfers between devices with their start and end apart: 9, of which 9 were waited for; matrix products, arithmetic and copies ran while one was open for 0% of the time, Pallas kernels for 0%

commit v1 on v0

--- a/solution.py
+++ b/solution.py
@@ -15,7 +15,15 @@
 def per_device(factor, right_side, occ_order, cabs_order):
     chain_size = lax.axis_size("chain")
     position = lax.axis_index("chain")
-    factor_row = lax.all_gather(factor, "cols", axis=0, tiled=True)
+    ways, here = (lax.axis_size("cols"), lax.axis_index("cols"))
+    grown, reach = (factor, 1)
+    while reach < ways:
+        theirs = lax.ppermute(grown, "cols", [(d, d ^ reach) for d in range(ways)])
+        mine_first = jnp.concatenate([grown, theirs], axis=0)
+        theirs_first = jnp.concatenate([theirs, grown], axis=0)
+        grown = jnp.where(here & reach == 0, mine_first, theirs_first)
+        reach = 2 * reach
+    factor_row = grown
     aux_rows = factor_row.shape[0]
     diag_block = lax.dynamic_slice_in_dim(factor_row, position * aux_rows, aux_rows, 1)
     identity = jnp.eye(aux_rows, dtype=jnp.float32)

time: 749 us -> 913 us (1.22)
  waiting for transfers between devices: 595 us -> 741 us
  other arithmetic: 61.4 us -> 80.3 us
  starting transfers between devices: 10.1 us -> 21.2 us
    ppermute x0 -> x5, waiting for transfers between devices: none -> 246 us  [per_device(): theirs = lax.ppermute(grown, 'cols', [(d, d ^ reach) for d in range(ways)])]
    all_gather x1 -> x0, waiting for transfers between devices: 128 us -> none  [per_device(): factor_row = lax.all_gather(factor, 'cols', axis=0, tiled=True)]
    all_gather x7, waiting for transfers between devices: 433 us -> 461 us  [from_root(): lax.all_gather(value, axis)]
    select_n x0 -> x5, other arithmetic: none -> 20.3 us  [per_device(): grown = jnp.where(here & reach == 0, mine_first, theirs_first)]
    ppermute x0 -> x5, starting transfers between devices: none -> 11.2 us  [per_device(): theirs = lax.ppermute(grown, 'cols', [(d, d ^ reach) for d in range(ways)])]
  transfers between devices with their start and end apart: 9 -> 13, of which waited for: 9 -> 13; matrix products, arithmetic and copies ran while one was open for 0% -> 0% of each run, Pallas kernels for 0% -> 0%
where the time goes in v1:
time: 913 us; the launch traced here: 909 us
  waiting for transfers between devices  741 us (81%)
  other arithmetic  80.3 us (9%)
  local copies, waits for them, and re-layouts  31.4 us (3%)
  starting transfers between devices  21.2 us (2%)
  matrix products  19.3 us (2%)
  between operations  14.1 us (2%)
    all_gather x7, waiting for transfers between devices, from_root(): lax.all_gather(value, axis)  461 us
    ppermute x5, waiting for transfers between devices, per_device(): theirs = lax.ppermute(grown, 'cols', [(d, d ^ reach) for d in range(ways)])  246 us
    another operation x7, other arithmetic, per_device(): jax.scipy.linalg.solve_triangular(diag_block, identity, lower=True)  51.3 us
    all_to_all x1, waiting for transfers between devices, per_device(): lax.all_to_all(grid, 'cols', split_axis=0, concat_axis=2, tiled=True)  34 us
    select_n x5, other arithmetic, per_device(): grown = jnp.where(here & reach == 0, mine_first, theirs_first)  20.3 us
    another operation x19, local copies, waits for them, and re-layouts  18.6 us
  transfers between devices with their start and end apart: 13, of which 13 were waited for; matrix products, arithmetic and copies ran while one was open for 0% of the time, Pallas kernels for 0%

profile of v1, /device:TPU:33, one launch (start us, length us, event | category | flops | bytes accessed | tf_op | source)
XLA Modules:
  0.0 908.9 jit_solution(4625729488481041979)
XLA Ops:
  6.5 1.3 copy.104
  7.9 11.0 %collective-permute-done = f32[18,4608]{1,0:T(8,128)S(1)} collective-permute-done((f32[18,4608]{1,0:T(8,128)S(1)}, f32[18,4608]{1,0:T(8,128)S(1)}, u32[]{:S(2)}, u32[]{:S(2)}) %collective-permute-start) | collective-permute-done | bytes 331808 | tf_op jit(solution)/shard_map/ppermute | solution.py:21
  19.1 3.1 collective-permute-start.1
  22.1 31.9 %collective-permute-done.1 = f32[36,4608]{1,0:T(8,128)} collective-permute-done((f32[36,4608]{1,0:T(8,128)S(1)}, f32[36,4608]{1,0:T(8,128)}, u32[]{:S(2)}, u32[]{:S(2)}) %collective-permute-start.1) | collective-permute-done | bytes 663584 | tf_op jit(solution)/shard_map/ppermute | solution.py:21
  54.1 1.5 maximum_select_fusion.3
  55.6 3.9 collective-permute-start.2
  59.5 35.7 %collective-permute-done.2 = f32[72,4608]{1,0:T(8,128)} collective-permute-done((f32[72,4608]{1,0:T(8,128)S(1)}, f32[72,4608]{1,0:T(8,128)}, u32[]{:S(2)}, u32[]{:S(2)}) %collective-permute-start.2) | collective-permute-done | bytes 1327136 | tf_op jit(solution)/shard_map/ppermute | solution.py:21
  95.1 3.6 maximum_select_fusion.2
  98.7 1.2 collective-permute-start.3
  99.9 56.7 %collective-permute-done.3 = f32[144,4608]{1,0:T(8,128)} collective-permute-done((f32[144,4608]{1,0:T(8,128)}, f32[144,4608]{1,0:T(8,128)}, u32[]{:S(2)}, u32[]{:S(2)}) %collective-permute-start.3) | collective-permute-done | bytes 2654240 | tf_op jit(solution)/shard_map/ppermute | solution.py:21
  156.6 6.4 maximum_select_fusion.1
  163.0 3.0 collective-permute-start.4
  166.2 1.3 fusion.68
  167.4 111.2 %collective-permute-done.4 = f32[288,4608]{1,0:T(8,128)} collective-permute-done((f32[288,4608]{1,0:T(8,128)}, f32[288,4608]{1,0:T(8,128)}, u32[]{:S(2)}, u32[]{:S(2)}) %collective-permute-start.4) | collective-permute-done | bytes 5308448 | tf_op jit(solution)/shard_map/ppermute | solution.py:21
  278.6 8.7 maximum_select_fusion
  287.3 4.0 copy-done
  291.7 10.4 %while.1 = (s32[]{:T(128)}, f32[576,576]{1,0:T(8,128)S(1)}, s32[4,2]{0,1:T(2,128)S(1)}, f32[4,128,128]{2,1,0:T(8,128)}, s32[]{:T(128)}) while((s32[]{:T(128)}, f32[576,576]{1,0:T(8,128)S(1)}, s32[4,2]{0,1:T(2,128)S(1)}, f32[4,128,128]{2,1,0:T(8,128)}, s32[]{:T(128)}) %tuple.161), condition=%wide.while_cond, body=%wide.while_body.sunk | while | flops 2 | bytes 132705 | solution.py:30
  292.3 2.0 bitcast_dynamic-update-slice_fusion.2
  294.9 2.0 bitcast_dynamic-update-slice_fusion.2
  297.5 2.0 bitcast_dynamic-update-slice_fusion.2
  300.0 2.0 bitcast_dynamic-update-slice_fusion.2
  302.1 1.2 pad_maximum_fusion
  303.3 49.8 %custom-call.4 = f32[5,128,128]{1,2,0:T(8,128)} custom-call(f32[5,128,128]{2,1,0:T(8,128)S(1)} %pad_maximum_fusion), custom_call_target="InvertDiagBlocksLowerTriangular" | custom-call | tf_op jit(solution)/shard_map/jit(_solve_triangular)/triangular_solve | solution.py:30
  353.1 1.2 constant_dynamic-update-slice_fusion.3
  354.3 1.4 convolution_subtract_fusion.1
  355.7 1.3 constant_dynamic-update-slice_fusion.2
  357.0 1.5 convolution_subtract_fusion
  359.0 1.9 convolution_subtract_fusion.2
  361.3 2.0 fusion.57
  363.6 1.2 conditional.15
  363.6 1.2 broadcast.60
  364.9 84.8 %all-gather.15.cloned.1.call-done = f32[4608,512]{1,0:T(8,128)} async-done(((f32[576,512]{1,0:T(8,128)}), f32[4608,512]{1,0:T(8,128)}) %all-gather.15.cloned.1.call-update) | async-done | bytes 9437200 | tf_op jit(solution)/shard_map/all_gather | solution.py:8
  449.6 5.3 conditional.16
  450.1 4.8 fusion.2
  454.9 4.1 conditional.17
  455.0 4.1 fusion.84
  459.1 55.5 %all-gather.17.cloned.1.call-done = f32[4608,512]{1,0:T(8,128)} async-done(((f32[576,512]{1,0:T(8,128)}), f32[4608,512]{1,0:T(8,128)}) %all-gather.17.cloned.1.call-update) | async-done | bytes 9437200 | tf_op jit(solution)/shard_map/all_gather | solution.py:8
  514.7 1.2 conditional.19
  514.7 1.2 broadcast.62
  515.9 63.7 %all-gather.19.cloned.1.call-done = f32[4608,512]{1,0:T(8,128)} async-done(((f32[576,512]{1,0:T(8,128)}), f32[4608,512]{1,0:T(8,128)}) %all-gather.19.cloned.1.call-update) | async-done | bytes 9437200 | tf_op jit(solution)/shard_map/all_gather | solution.py:8
  579.8 1.2 conditional.21
  579.8 1.2 broadcast.63
  581.0 63.4 %all-gather.21.cloned.1.call-done = f32[4608,512]{1,0:T(8,128)} async-done(((f32[576,512]{1,0:T(8,128)}), f32[4608,512]{1,0:T(8,128)}) %all-gather.21.cloned.1.call-update) | async-done | bytes 9437200 | tf_op jit(solution)/shard_map/all_gather | solution.py:8
  644.4 1.3 conditional.23
  644.4 1.3 broadcast.64
  645.8 64.9 %all-gather.23.cloned.1.call-done = f32[4608,512]{1,0:T(8,128)} async-done(((f32[576,512]{1,0:T(8,128)}), f32[4608,512]{1,0:T(8,128)}) %all-gather.23.cloned.1.call-update) | async-done | bytes 9437200 | tf_op jit(solution)/shard_map/all_gather | solution.py:8
  710.9 1.2 conditional.25
  710.9 1.2 broadcast.65
  712.1 64.6 %all-gather.25.cloned.1.call-done = f32[4608,512]{1,0:T(8,128)} async-done(((f32[576,512]{1,0:T(8,128)}), f32[4608,512]{1,0:T(8,128)}) %all-gather.25.cloned.1.call-update) | async-done | bytes 9437200 | tf_op jit(solution)/shard_map/all_gather | solution.py:8
  776.8 1.2 conditional.27
  776.8 1.2 broadcast.66
  778.2 63.8 %all-gather.27.cloned.1.call-done = f32[4608,512]{1,0:T(8,128)} async-done(((f32[576,512]{1,0:T(8,128)}), f32[4608,512]{1,0:T(8,128)}) %all-gather.27.cloned.1.call-update) | async-done | bytes 9437200 | tf_op jit(solution)/shard_map/all_gather | solution.py:8
  842.4 1.2 conditional.29
  842.4 1.2 broadcast.67
  843.6 4.9 add_add_fusion
  848.8 0.8 copy.46
  849.6 0.7 gather_fusion
  850.3 1.2 select_bitcast_fusion.1
  851.5 9.8 %all-to-all-start = ((f32[32,2,8,576]{3,2,1,0:T(8,128)}), f32[32,2,8,576]{3,2,1,0:T(8,128)S(1)}, u32[]{:S(2)}, u32[]{:S(2)}) async-start(f32[32,2,8,576]{3,2,1,0:T(8,128)} %select_bitcast_fusion.1), calls=%async_computation | async-start | bytes 2621440 | tf_op jit(solution)/shard_map/all_to_all | solution.py:63
  861.3 34.0 %all-to-all-done = f32[32,2,8,576]{3,2,1,0:T(8,128)S(1)} async-done(((f32[32,2,8,576]{3,2,1,0:T(8,128)}), f32[32,2,8,576]{3,2,1,0:T(8,128)S(1)}, u32[]{:S(2)}, u32[]{:S(2)}) %all-to-all-start) | async-done | bytes 1179680 | tf_op jit(solution)/shard_map/all_to_all | solution.py:63
  895.4 1.0 copy.48
  896.4 2.2 gather_fusion.1
  898.5 1.1 select_bitcast_fusion
  899.7 2.2 copy.49
  (63 shorter events, 6.0 us)
Async XLA Ops:
  6.5 1.4 copy-start.3
  6.5 443.1 %all-gather.15.cloned.1.call-start = ((), (), s32[]{:S(2)}) async-start(), calls=%async_computation.1 | async-start | bytes 10616832 | tf_op jit(solution)/shard_map/all_gather | solution.py:8
  7.9 11.0 %collective-permute-start = (f32[18,4608]{1,0:T(8,128)S(1)}, f32[18,4608]{1,0:T(8,128)S(1)}, u32[]{:S(2)}, u32[]{:S(2)}) collective-permute-start(f32[18,4608]{1,0:T(8,128)S(1)} %copy-done.3), channel_id=1, source_target_pairs={{0,1},{1,0},{2,3},{3,2},{4,5},{5,4},{6,7},{7,6},{8,9},{9,8},{10,11... | collective-permute-start | bytes 995336 | tf_op jit(solution)/shard_map/ppermute | solution.py:21
  19.1 35.0 %collective-permute-start.1 = (f32[36,4608]{1,0:T(8,128)S(1)}, f32[36,4608]{1,0:T(8,128)}, u32[]{:S(2)}, u32[]{:S(2)}) collective-permute-start(f32[36,4608]{1,0:T(8,128)S(1)} %maximum_select_fusion.4), channel_id=1, source_target_pairs={{0,2},{1,3},{2,0},{3,1},{4,6},{5,7},{6,4},{7,5},{8,10},{9,11},{10,... | collective-permute-start | bytes 1990664 | tf_op jit(solution)/shard_map/ppermute | solution.py:21
  55.6 39.5 %collective-permute-start.2 = (f32[72,4608]{1,0:T(8,128)S(1)}, f32[72,4608]{1,0:T(8,128)}, u32[]{:S(2)}, u32[]{:S(2)}) collective-permute-start(f32[72,4608]{1,0:T(8,128)S(1)} %maximum_select_fusion.3), channel_id=1, source_target_pairs={{0,4},{1,5},{2,6},{3,7},{4,0},{5,1},{6,2},{7,3},{8,12},{9,13},{10,... | collective-permute-start | bytes 3981320 | tf_op jit(solution)/shard_map/ppermute | solution.py:21
  98.7 57.9 %collective-permute-start.3 = (f32[144,4608]{1,0:T(8,128)}, f32[144,4608]{1,0:T(8,128)}, u32[]{:S(2)}, u32[]{:S(2)}) collective-permute-start(f32[144,4608]{1,0:T(8,128)} %maximum_select_fusion.2), channel_id=1, source_target_pairs={{0,8},{1,9},{2,10},{3,11},{4,12},{5,13},{6,14},{7,15},{8,0},{9,1},... | collective-permute-start | bytes 7962632 | tf_op jit(solution)/shard_map/ppermute | solution.py:21
  163.0 115.6 %collective-permute-start.4 = (f32[288,4608]{1,0:T(8,128)}, f32[288,4608]{1,0:T(8,128)}, u32[]{:S(2)}, u32[]{:S(2)}) collective-permute-start(f32[288,4608]{1,0:T(8,128)} %maximum_select_fusion.1), channel_id=1, source_target_pairs={{0,16},{1,17},{2,18},{3,19},{4,20},{5,21},{6,22},{7,23},{8,24},{9,... | collective-permute-start | bytes 15925256 | tf_op jit(solution)/shard_map/ppermute | solution.py:21
  287.3 4.1 copy-start
  302.0 1.3 copy-start.2
  353.1 4.0 copy-start.1
  355.7 2.9 copy-start.4
  364.8 149.8 %all-gather.17.cloned.1.call-start = ((), (), s32[]{:S(2)}) async-start(), calls=%async_computation.2 | async-start | bytes 10616832 | tf_op jit(solution)/shard_map/all_gather | solution.py:8
  459.1 120.5 %all-gather.19.cloned.1.call-start = ((), (), s32[]{:S(2)}) async-start(), calls=%async_computation.3 | async-start | bytes 10616832 | tf_op jit(solution)/shard_map/all_gather | solution.py:8
  515.9 128.5 %all-gather.21.cloned.1.call-start = ((), (), s32[]{:S(2)}) async-start(), calls=%async_computation.4 | async-start | bytes 10616832 | tf_op jit(solution)/shard_map/all_gather | solution.py:8
  581.0 129.7 %all-gather.23.cloned.1.call-start = ((), (), s32[]{:S(2)}) async-start(), calls=%async_computation.5 | async-start | bytes 10616832 | tf_op jit(solution)/shard_map/all_gather | solution.py:8
  645.7 131.1 %all-gather.25.cloned.1.call-start = ((), (), s32[]{:S(2)}) async-start(), calls=%async_computation.6 | async-start | bytes 10616832 | tf_op jit(solution)/shard_map/all_gather | solution.py:8
  712.1 129.9 %all-gather.27.cloned.1.call-start = ((), (), s32[]{:S(2)}) async-start(), calls=%async_computation.7 | async-start | bytes 10616832 | tf_op jit(solution)/shard_map/all_gather | solution.py:8
  776.8 1.2 copy-start.6
  776.8 1.3 copy-start.5
  851.5 43.8 %all-to-all-start = ((f32[32,2,8,576]{3,2,1,0:T(8,128)}), f32[32,2,8,576]{3,2,1,0:T(8,128)S(1)}, u32[]{:S(2)}, u32[]{:S(2)}) async-start(f32[32,2,8,576]{3,2,1,0:T(8,128)} %select_bitcast_fusion.1), calls=%async_computation | async-start | bytes 2621440 | tf_op jit(solution)/shard_map/all_to_all | solution.py:63
Sparse Core Ops, SparseCore 0:
  364.9 84.6 all-gather.14
  459.2 55.4 all-gather.16
  516.5 63.0 all-gather.18
  581.3 63.0 all-gather.20
  646.1 64.5 all-gather.22
  712.4 64.3 all-gather.24
  778.6 63.3 all-gather.26
